TPU v7x, 256 devices: a whole 4x4x8 slice. The times are simulated.
256 devices in a mesh: pl: 16 (over y, x), xs: 16 (over z, core).
Axes of the slice: x: 4, y: 4, z: 8, core: 2. Of those that a mesh axis runs over, the one named last changes fastest.
Arguments:
- source: float32 [512, 16, 2048], P('xs', None, 'pl'), may hold values from -6 to 6
- eastward_rate: float32 [512, 16, 2048], P('xs', None, 'pl'), may hold values from 300 to 6000
- northward_rate: float32 [512, 16, 2048], P('xs', None, 'pl'), may hold values from 300 to 6000
- vertical_rate: float32 [512, 16, 2048], P('xs', None, 'pl'), may hold values from 0.5 to 20
- amplitude: float32 [512, 16, 2048], P('xs', None, 'pl'), may hold values from 300 to 3000
Outputs:
- smoothed: float32 [512, 16, 2048], P('xs', None, 'pl')
All inputs are finite; a program needn't handle non-finite values.
Results may differ from a plain program's by a relative error of at most 0.0003.
Values sent between devices are 32-bit elements; how exact they have to be, the bound alone decides.
A program may use at most 128 MiB of HBM per device.

v0:
```python
import jax
import jax.numpy as jnp
from jax import lax
from jax.sharding import PartitionSpec as P


def cyclic(sub_band, centre, super_band, values):
    length = centre.shape[0]
    if length == 1:
        return values / centre

    def halves(operand):
        paired = operand.reshape((length // 2, 2) + operand.shape[1:])
        return (paired[:, 0], paired[:, 1])

    def following(operand, filler):
        return jnp.concatenate([operand[1:], jnp.full_like(operand[:1], filler)], axis=0)

    sub_even, sub_odd = halves(sub_band)
    centre_even, centre_odd = halves(centre)
    super_even, super_odd = halves(super_band)
    values_even, values_odd = halves(values)
    left_factor = -sub_odd / centre_even
    right_factor = -super_odd / following(centre_even, 1.0)
    reduced = cyclic(
        left_factor * sub_even,
        centre_odd + left_factor * super_even + right_factor * following(sub_even, 0.0),
        right_factor * following(super_even, 0.0),
        values_odd + left_factor * values_even + right_factor * following(values_even, 0.0),
    )
    previous = jnp.concatenate([jnp.zeros_like(reduced[:1]), reduced[:-1]], axis=0)
    even_part = (values_even - sub_even * previous - super_even * reduced) / centre_even
    return jnp.stack([even_part, reduced], axis=1).reshape((length,) + even_part.shape[1:])


def cyclic_last(sub_band, centre, super_band, values):
    length = centre.shape[-1]
    if length == 1:
        return values / centre

    def halves(operand):
        paired = operand.reshape(operand.shape[:-1] + (length // 2, 2))
        return (paired[..., 0], paired[..., 1])

    def following(operand, filler):
        return jnp.concatenate([operand[..., 1:], jnp.full_like(operand[..., :1], filler)], axis=-1)

    sub_even, sub_odd = halves(sub_band)
    centre_even, centre_odd = halves(centre)
    super_even, super_odd = halves(super_band)
    values_even, values_odd = halves(values)
    left_factor = -sub_odd / centre_even
    right_factor = -super_odd / following(centre_even, 1.0)
    reduced = cyclic_last(
        left_factor * sub_even,
        centre_odd + left_factor * super_even + right_factor * following(sub_even, 0.0),
        right_factor * following(super_even, 0.0),
        values_odd + left_factor * values_even + right_factor * following(values_even, 0.0),
    )
    previous = jnp.concatenate([jnp.zeros_like(reduced[..., :1]), reduced[..., :-1]], axis=-1)
    even_part = (values_even - sub_even * previous - super_even * reduced) / centre_even
    return jnp.stack([even_part, reduced], axis=-1).reshape(even_part.shape[:-1] + (length,))


def band_solve(values, rate_lines):
    length = values.shape[0]
    position = lax.broadcasted_iota(jnp.int32, rate_lines.shape, 0)
    sub_band = jnp.where(position > 0, -rate_lines, 0.0)
    super_band = jnp.where(position < length - 1, -rate_lines, 0.0)
    return cyclic(sub_band, 1.0 + 2.0 * rate_lines, super_band, values)


def vertical_solve(values, vertical_lines):
    return jnp.moveaxis(band_solve(jnp.moveaxis(values, 1, 0), vertical_lines), 0, 1)


def northward_solve(values, north_lines):
    length = values.shape[-1]
    position = lax.broadcasted_iota(jnp.int32, north_lines.shape, 2)
    sub_band = jnp.where(position > 0, -north_lines, 0.0)
    super_band = jnp.where(position < length - 1, -north_lines, 0.0)
    return cyclic_last(sub_band, 1.0 + 2.0 * north_lines, super_band, values)


def to_lines(values):
    return lax.all_to_all(values, "pl", split_axis=1, concat_axis=2, tiled=True)


def to_planes(values):
    return lax.all_to_all(values, "pl", split_axis=2, concat_axis=1, tiled=True)


def matrix_product(left_matrix, right_matrix):
    return (
        left_matrix[0] * right_matrix[0] + left_matrix[1] * right_matrix[2],
        left_matrix[0] * right_matrix[1] + left_matrix[1] * right_matrix[3],
        left_matrix[2] * right_matrix[0] + left_matrix[3] * right_matrix[2],
        left_matrix[2] * right_matrix[1] + left_matrix[3] * right_matrix[3],
    )


def matrix_inverse(matrix):
    determinant = matrix[0] * matrix[3] - matrix[1] * matrix[2]
    return (
        matrix[3] / determinant,
        -matrix[1] / determinant,
        -matrix[2] / determinant,
        matrix[0] / determinant,
    )


def matrix_vector(matrix, vector):
    return (
        matrix[0] * vector[0] + matrix[1] * vector[1],
        matrix[2] * vector[0] + matrix[3] * vector[1],
    )


def unpack_rows(packed):
    sub_block = (packed[0], packed[1], packed[2], packed[3])
    centre = (packed[4] + 1.0, packed[5], packed[6], packed[7] + 1.0)
    super_block = (packed[8], packed[9], packed[10], packed[11])
    right_side = (packed[12], packed[13])
    return (sub_block, centre, super_block, right_side)


def pack_rows(sub_block, centre, super_block, right_side):
    return jnp.stack(
        [
            sub_block[0],
            sub_block[1],
            sub_block[2],
            sub_block[3],
            centre[0] - 1.0,
            centre[1],
            centre[2],
            centre[3] - 1.0,
            super_block[0],
            super_block[1],
            super_block[2],
            super_block[3],
            right_side[0],
            right_side[1],
        ]
    )


def first_rows(boundary):
    blank_rows = jnp.zeros_like(boundary[0])
    return jnp.stack(
        [
            blank_rows,
            boundary[0],
            blank_rows,
            boundary[1],
            blank_rows,
            blank_rows,
            blank_rows,
            blank_rows,
            boundary[2],
            blank_rows,
            boundary[3],
            blank_rows,
            boundary[4],
            boundary[5],
        ]
    )


def eliminate(own_rows, rows_below, rows_above):
    sub_block, centre, super_block, right_side = unpack_rows(own_rows)
    sub_below, centre_below, super_below, right_below = unpack_rows(rows_below)
    sub_above, centre_above, super_above, right_above = unpack_rows(rows_above)
    left_factor = matrix_product(sub_block, matrix_inverse(centre_below))
    right_factor = matrix_product(super_block, matrix_inverse(centre_above))
    new_sub = tuple((-entry for entry in matrix_product(left_factor, sub_below)))
    new_super = tuple((-entry for entry in matrix_product(right_factor, super_above)))
    left_part = matrix_product(left_factor, super_below)
    right_part = matrix_product(right_factor, sub_above)
    new_centre = tuple((centre[slot] - left_part[slot] - right_part[slot] for slot in range(4)))
    left_vector = matrix_vector(left_factor, right_below)
    right_vector = matrix_vector(right_factor, right_above)
    new_right = (
        right_side[0] - left_vector[0] - right_vector[0],
        right_side[1] - left_vector[1] - right_vector[1],
    )
    return pack_rows(new_sub, new_centre, new_super, new_right)


def finish_rows(packed):
    sub_block, centre, super_block, right_side = unpack_rows(packed)
    return matrix_vector(matrix_inverse(centre), right_side)


def solve_gathered(gathered, own_index, devices):
    row_blocks = first_rows(jnp.moveaxis(gathered, 0, 1))
    stride = 1
    while stride < devices:
        blank_rows = jnp.zeros_like(row_blocks[:, :stride])
        rows_below = jnp.concatenate([blank_rows, row_blocks[:, :-stride]], axis=1)
        rows_above = jnp.concatenate([row_blocks[:, stride:], blank_rows], axis=1)
        row_blocks = eliminate(row_blocks, rows_below, rows_above)
        stride = stride * 2
    first_value, last_value = finish_rows(row_blocks)
    blank_value = jnp.zeros_like(first_value[:1])
    padded_first = jnp.concatenate([blank_value, first_value, blank_value], axis=0)
    padded_last = jnp.concatenate([blank_value, last_value, blank_value], axis=0)
    last_before = lax.dynamic_index_in_dim(padded_last, own_index, 0, keepdims=False)
    first_after = lax.dynamic_index_in_dim(padded_first, own_index + 2, 0, keepdims=False)
    return (last_before, first_after)


def coupled(boundary):
    devices = lax.axis_size("xs")
    gathered = lax.all_gather(boundary[None], "xs", axis=0, tiled=True)
    last_before, first_after = solve_gathered(gathered, lax.axis_index("xs"), devices)
    return (last_before, first_after)


def spike_parts(values, rate, own_index, devices):
    length = values.shape[0]
    position = lax.broadcasted_iota(jnp.int32, values.shape, 0)
    sub_band = jnp.where(position > 0, -rate, 0.0)
    super_band = jnp.where(position < length - 1, -rate, 0.0)
    centre = 1.0 + 2.0 * rate
    left_edge = jnp.where((position == 0) & (own_index > 0), -rate, 0.0)
    right_edge = jnp.where((position == length - 1) & (own_index < devices - 1), -rate, 0.0)
    stacked = jnp.stack([values, left_edge, right_edge], axis=1)
    solved = cyclic(sub_band[:, None], centre[:, None], super_band[:, None], stacked)
    particular = solved[:, 0]
    spike_left = solved[:, 1]
    spike_right = solved[:, 2]
    boundary = jnp.stack(
        [
            spike_left[0],
            spike_left[-1],
            spike_right[0],
            spike_right[-1],
            particular[0],
            particular[-1],
        ]
    )
    return (particular, spike_left, spike_right, boundary)


def eastward_solve(values, east_rate):
    particular, spike_left, spike_right, boundary = spike_parts(
        values, east_rate, lax.axis_index("xs"), lax.axis_size("xs")
    )
    last_before, first_after = coupled(boundary)
    return particular - spike_left * last_before[None] - spike_right * first_after[None]


def shards(source, eastward_rate, northward_rate, vertical_rate, amplitude):
    vertical_lines = jnp.moveaxis(vertical_rate, 1, 0)
    values = vertical_solve(source, vertical_lines)
    north_lines = lax.all_to_all(northward_rate, "pl", split_axis=1, concat_axis=2, tiled=True)
    values = to_planes(northward_solve(to_lines(values), north_lines))
    values = eastward_solve(values, eastward_rate)
    values = eastward_solve(values, eastward_rate)
    values = to_planes(northward_solve(to_lines(values), north_lines))
    values = vertical_solve(values, vertical_lines)
    return amplitude * values


def solution(mesh):
    placed = (
        P("xs", None, "pl"),
        P("xs", None, "pl"),
        P("xs", None, "pl"),
        P("xs", None, "pl"),
        P("xs", None, "pl"),
    )
    return jax.shard_map(
        shards, mesh=mesh, in_specs=placed, out_specs=P("xs", None, "pl"), check_vma=False
    )
```

profile of v0, /device:TPU:32, one launch (start us, length us, event | category | flops | bytes accessed | tf_op | source)
XLA Modules:
  0.0 218.9 jit_solution(4738351005885732317)
XLA Ops:
  3.7 7.0 %all-to-all-start = ((f32[32,16,128]{2,0,1:T(8,128)}), f32[32,16,128]{2,0,1:T(8,128)S(1)}, u32[]{:S(2)}, u32[]{:S(2)}) async-start(f32[32,16,128]{2,0,1:T(8,128)} %bitcast.68), calls=%async_computation | async-start | bytes 524288 | tf_op jit(solution)/shard_map/all_to_all | solution.py:86
  27.6 7.4 %all-to-all-start.1 = ((f32[32,16,128]{2,0,1:T(8,128)}), f32[32,16,128]{2,0,1:T(8,128)S(1)}, u32[]{:S(2)}, u32[]{:S(2)}) async-start(f32[32,16,128]{2,0,1:T(8,128)} %copy.1550), calls=%async_computation.1 | async-start | bytes 524288 | tf_op jit(solution)/shard_map/all_to_all | solution.py:257
  35.3 1.6 fusion.580
  37.8 5.9 %all-to-all-done.1 = f32[32,16,128]{2,0,1:T(8,128)S(1)} async-done(((f32[32,16,128]{2,0,1:T(8,128)}), f32[32,16,128]{2,0,1:T(8,128)S(1)}, u32[]{:S(2)}, u32[]{:S(2)}) %all-to-all-start.1) | async-done | bytes 262176 | tf_op jit(solution)/shard_map/all_to_all | solution.py:257
  44.1 1.6 fusion.579
  47.2 2.6 %copy_select_fusion = (f32[32,1,1024,2]{0,2,3,1:T(8,128)S(1)}, f32[32,1,1024,2]{0,2,3,1:T(8,128)S(1)}) fusion(f32[32,1,1024,2]{0,3,2,1:T(2,128)} %bitcast.4710, pred[1024,2]{0,1:T(4,128)(4,1)S(1)} %get-tuple-element.502, pred[1024,2]{0,1:T(4,128)(4,1)S(1)} %get-tuple-element.503), kind=kLoop, calls=%fused_computation.210 | loop fusion | flops 131072 | bytes 790528 | tf_op jit(solution)/shard_map/jit(_where)/select_n | solution.py:81
  61.8 1.9 copy.1628
  64.2 11.6 %reduce = f32[2048,32]{1,0:T(8,128)} reduce(f32[2048,1,32]{2,1,0:T(1,128)} %bitcast.4714, f32[]{:T(128)} %broadcast.2033), dimensions={1}, to_apply=%bitcast.4048.reduce_sub_computation | reduce | bytes 524292
  75.8 2.4 %reshape.3598 = f32[16,1,4096]{2,1,0:T(1,128)} reshape(f32[2048,32]{1,0:T(8,128)} %reduce) | data formatting | bytes 524288
  78.2 4.2 %all-to-all-start.2 = ((f32[16,1,4096]{2,1,0:T(1,128)}), f32[16,1,4096]{2,1,0:T(1,128)}, u32[]{:S(2)}, u32[]{:S(2)}) async-start(f32[16,1,4096]{2,1,0:T(1,128)} %reshape.3598), calls=%async_computation.2 | async-start | bytes 524288 | tf_op jit(solution)/shard_map/all_to_all | solution.py:90
  85.1 1.8 bitcast_divide_fusion.61
  86.9 4.2 %all-to-all-done.2 = f32[16,1,4096]{2,1,0:T(1,128)} async-done(((f32[16,1,4096]{2,1,0:T(1,128)}), f32[16,1,4096]{2,1,0:T(1,128)}, u32[]{:S(2)}, u32[]{:S(2)}) %all-to-all-start.2) | async-done | bytes 262176 | tf_op jit(solution)/shard_map/all_to_all | solution.py:90
  91.1 2.9 %reduce.1 = f32[16,4096]{1,0:T(8,128)} reduce(f32[16,1,4096]{2,1,0:T(1,128)} %all-to-all-done.2, f32[]{:T(128)} %broadcast.2033), dimensions={1}, to_apply=%all_to_all.14.reduce_sub_computation | reduce | bytes 524292 | tf_op jit(solution)/shard_map/all_to_all | solution.py:90
  93.9 3.7 %reshape.3599 = f32[2048,1,32]{2,1,0:T(1,128)} reshape(f32[16,4096]{1,0:T(8,128)} %reduce.1) | data formatting | bytes 524288
  97.7 3.4 %copy.1630 = f32[32,1,2048]{2,1,0:T(1,128)} copy(f32[32,1,2048]{0,1,2:T(1,128)} %bitcast.4711) | data formatting | bytes 524288 | tf_op jit(solution)/shard_map/all_to_all | solution.py:90
  104.9 20.5 %all-gather = f32[96,16,128]{2,1,0:T(8,128)S(1)} all-gather(f32[6,16,128]{2,1,0:T(8,128)S(1)} %constant_dynamic-update-slice_fusion), channel_id=2, replica_groups=mesh['pl'=16,'xs'=16] {'xs'}, dimensions={0}, use_global_device_ids=true | all-gather | bytes 835584 | tf_op jit(solution)/shard_map/all_gather | solution.py:215
  130.9 5.1 %fusion.406 = (f32[16,16,128]{2,1,0:T(8,128)S(1)}, f32[16,16,128]{2,1,0:T(8,128)S(1)}, f32[16,16,128]{2,1,0:T(8,128)S(1)}, f32[16,16,128]{2,1,0:T(8,128)S(1)}, f...) fusion(f32[16,16,128]{2,1,0:T(8,128)S(1)} %get-tuple-element.322, ...), kind=kLoop, calls=%fused_computation.1275 | loop fusion | flops 23101440 | bytes 16613376 | tf_op jit(solution)/shard_map/add | solution.py:115
  138.8 18.6 %all-gather.1 = f32[96,16,128]{2,1,0:T(8,128)S(1)} all-gather(f32[6,16,128]{2,1,0:T(8,128)S(1)} %constant_dynamic-update-slice_fusion.56), channel_id=3, replica_groups=mesh['pl'=16,'xs'=16] {'xs'}, dimensions={0}, use_global_device_ids=true | all-gather | bytes 835584 | tf_op jit(solution)/shard_map/all_gather | solution.py:215
  162.9 5.0 %fusion.403 = (f32[16,16,128]{2,1,0:T(8,128)S(1)}, f32[16,16,128]{2,1,0:T(8,128)S(1)}, f32[16,16,128]{2,1,0:T(8,128)S(1)}, f32[16,16,128]{2,1,0:T(8,128)S(1)}, f...) fusion(f32[16,16,128]{2,1,0:T(8,128)S(1)} %get-tuple-element.316, ...), kind=kLoop, calls=%fused_computation.1183 | loop fusion | flops 23101440 | bytes 16613376 | tf_op jit(solution)/shard_map/add | solution.py:115
  168.2 12.3 %all_to_all.23 = f32[32,16,128]{2,0,1:T(8,128)S(1)} all-to-all(f32[32,16,128]{2,0,1:T(8,128)S(1)} %copy.1714), channel_id=1, replica_groups=mesh['pl'=16,'xs'=16] {'pl'}, dimensions={1} | all-to-all | bytes 524288 | tf_op jit(solution)/shard_map/all_to_all | solution.py:86
  181.8 2.5 %fusion.578 = (f32[32,1,1024,1]{0,3,2,1:T(1,128)S(1)}, f32[32,1,1024,1]{0,3,2,1:T(1,128)S(1)}) fusion(f32[32,1,1024,2]{0,3,2,1:T(2,128)} %bitcast.4715), kind=kLoop, calls=%fused_computation.1763 | loop fusion | bytes 524288 | tf_op jit(solution)/shard_map/slice | solution.py:43
  190.6 9.3 %reduce.2 = f32[2048,32]{1,0:T(8,128)S(1)} reduce(f32[2048,1,32]{2,1,0:T(1,128)S(1)} %bitcast.4716, f32[]{:T(128)} %broadcast.2033), dimensions={1}, to_apply=%bitcast.4050.reduce_sub_computation | reduce | bytes 524292
  200.4 11.8 %all_to_all.24 = f32[16,1,4096]{2,1,0:T(1,128)S(1)} all-to-all(f32[16,1,4096]{2,1,0:T(1,128)S(1)} %reshape.3600), channel_id=1, replica_groups=mesh['pl'=16,'xs'=16] {'pl'}, dimensions={0} | all-to-all | bytes 524288 | tf_op jit(solution)/shard_map/all_to_all | solution.py:90
  213.4 1.8 reshape.3601
  (894 shorter events, 63.7 us)
Async XLA Ops:
  2.3 8.4 %copy-start.113 = (f32[32,16,128]{2,1,0:T(8,128)S(1)}, f32[32,16,128]{2,1,0:T(8,128)}, u32[]{:S(2)}) copy-start(f32[32,16,128]{2,1,0:T(8,128)} %param.6) | copy-start | bytes 786436
  3.7 23.9 %all-to-all-start = ((f32[32,16,128]{2,0,1:T(8,128)}), f32[32,16,128]{2,0,1:T(8,128)S(1)}, u32[]{:S(2)}, u32[]{:S(2)}) async-start(f32[32,16,128]{2,0,1:T(8,128)} %bitcast.68), calls=%async_computation | async-start | bytes 524288 | tf_op jit(solution)/shard_map/all_to_all | solution.py:86
  13.6 12.6 %copy-start.112 = (f32[32,16,128]{2,1,0:T(8,128)S(1)}, f32[32,16,128]{2,1,0:T(8,128)}, u32[]{:S(2)}) copy-start(f32[32,16,128]{2,1,0:T(8,128)} %param.7) | copy-start | bytes 786436
  27.6 16.1 %all-to-all-start.1 = ((f32[32,16,128]{2,0,1:T(8,128)}), f32[32,16,128]{2,0,1:T(8,128)S(1)}, u32[]{:S(2)}, u32[]{:S(2)}) async-start(f32[32,16,128]{2,0,1:T(8,128)} %copy.1550), calls=%async_computation.1 | async-start | bytes 524288 | tf_op jit(solution)/shard_map/all_to_all | solution.py:257
  52.8 8.1 %copy-start.2 = (f32[32,1,512,1]{0,3,2,1:T(1,128)}, f32[32,1,512,1]{0,3,2,1:T(1,128)S(1)}, u32[]{:S(2)}) copy-start(f32[32,1,512,1]{0,3,2,1:T(1,128)S(1)} %get-tuple-element.347) | copy-start | bytes 196612
  53.3 7.6 %copy-start.4 = (f32[32,1,512,1]{0,3,2,1:T(1,128)}, f32[32,1,512,1]{0,3,2,1:T(1,128)S(1)}, u32[]{:S(2)}) copy-start(f32[32,1,512,1]{0,3,2,1:T(1,128)S(1)} %get-tuple-element.343) | copy-start | bytes 196612
  54.6 5.9 %copy-start.16 = (f32[32,1,256,1]{0,3,2,1:T(1,128)}, f32[32,1,256,1]{0,3,2,1:T(1,128)S(1)}, u32[]{:S(2)}) copy-start(f32[32,1,256,1]{0,3,2,1:T(1,128)S(1)} %get-tuple-element.372) | copy-start | bytes 98308
  54.8 5.7 %copy-start.18 = (f32[32,1,256,1]{0,3,2,1:T(1,128)}, f32[32,1,256,1]{0,3,2,1:T(1,128)S(1)}, u32[]{:S(2)}) copy-start(f32[32,1,256,1]{0,3,2,1:T(1,128)S(1)} %get-tuple-element.368) | copy-start | bytes 98308
  55.3 5.0 %copy-start.14 = (f32[32,1,128,1]{0,3,2,1:T(1,128)}, f32[32,1,128,1]{0,3,2,1:T(1,128)S(1)}, u32[]{:S(2)}) copy-start(f32[32,1,128,1]{0,3,2,1:T(1,128)S(1)} %get-tuple-element.399) | copy-start | bytes 49156
  55.7 4.6 %copy-start.41 = (f32[32,1,128,1]{0,3,2,1:T(1,128)}, f32[32,1,128,1]{0,3,2,1:T(1,128)S(1)}, u32[]{:S(2)}) copy-start(f32[32,1,128,1]{0,3,2,1:T(1,128)S(1)} %get-tuple-element.400) | copy-start | bytes 49156
  55.8 4.5 %copy-start.43 = (f32[32,1,128,1]{0,3,2,1:T(1,128)}, f32[32,1,128,1]{0,3,2,1:T(1,128)S(1)}, u32[]{:S(2)}) copy-start(f32[32,1,128,1]{0,3,2,1:T(1,128)S(1)} %get-tuple-element.396) | copy-start | bytes 49156
  56.1 4.0 %copy-start.35 = (f32[32,1,64,1]{0,3,2,1:T(1,128)}, f32[32,1,64,1]{0,3,2,1:T(1,128)S(1)}, u32[]{:S(2)}) copy-start(f32[32,1,64,1]{0,3,2,1:T(1,128)S(1)} %get-tuple-element.417) | copy-start | bytes 24580
  56.6 3.6 %copy-start.67 = (f32[32,1,64,1]{0,3,2,1:T(1,128)}, f32[32,1,64,1]{0,3,2,1:T(1,128)S(1)}, u32[]{:S(2)}) copy-start(f32[32,1,64,1]{0,3,2,1:T(1,128)S(1)} %get-tuple-element.418) | copy-start | bytes 24580
  56.6 3.6 %copy-start.71 = (f32[32,1,64,1]{0,3,2,1:T(1,128)}, f32[32,1,64,1]{0,3,2,1:T(1,128)S(1)}, u32[]{:S(2)}) copy-start(f32[32,1,64,1]{0,3,2,1:T(1,128)S(1)} %get-tuple-element.419) | copy-start | bytes 24580
  56.7 3.7 %copy-start.69 = (f32[32,1,64,1]{0,3,2,1:T(1,128)}, f32[32,1,64,1]{0,3,2,1:T(1,128)S(1)}, u32[]{:S(2)}) copy-start(f32[32,1,64,1]{0,3,2,1:T(1,128)S(1)} %get-tuple-element.414) | copy-start | bytes 24580
  56.7 3.7 %copy-start.100 = (f32[32,1,64]{0,2,1:T(8,128)}, f32[32,1,64]{0,2,1:T(8,128)S(1)}, u32[]{:S(2)}) copy-start(f32[32,1,64]{0,2,1:T(8,128)S(1)} %get-tuple-element.236) | copy-start | bytes 24580
  56.9 3.2 %copy-start.88 = (f32[32,1,32,1]{0,3,2,1:T(1,128)}, f32[32,1,32,1]{0,3,2,1:T(1,128)S(1)}, u32[]{:S(2)}) copy-start(f32[32,1,32,1]{0,3,2,1:T(1,128)S(1)} %get-tuple-element.434) | copy-start | bytes 12292
  64.2 18.8 %copy-start.60 = (f32[16,1,1,16,128]{4,1,0,3,2:T(1,128)S(1)}, f32[16,1,1,16,128]{4,1,0,3,2:T(1,128)}, u32[]{:S(2)}) copy-start(f32[16,1,1,16,128]{4,1,0,3,2:T(1,128)} %copy-done.59) | copy-start | bytes 393220
  64.2 19.5 %copy-start.64 = (f32[32,16,128]{2,0,1:T(8,128)S(1)}, f32[32,16,128]{2,0,1:T(8,128)}, u32[]{:S(2)}) copy-start(f32[32,16,128]{2,0,1:T(8,128)} %get-tuple-element.364) | copy-start | bytes 786436
  78.2 12.9 %all-to-all-start.2 = ((f32[16,1,4096]{2,1,0:T(1,128)}), f32[16,1,4096]{2,1,0:T(1,128)}, u32[]{:S(2)}, u32[]{:S(2)}) async-start(f32[16,1,4096]{2,1,0:T(1,128)} %reshape.3598), calls=%async_computation.2 | async-start | bytes 524288 | tf_op jit(solution)/shard_map/all_to_all | solution.py:90
  83.9 17.2 %copy-start.30 = (f32[32,16,128]{2,1,0:T(8,128)}, f32[32,16,128]{2,1,0:T(8,128)S(1)}, u32[]{:S(2)}) copy-start(f32[32,16,128]{2,1,0:T(8,128)S(1)} %copy.1633) | copy-start | bytes 786436
  85.1 17.0 %copy-start.32 = (f32[32,16,128]{2,1,0:T(8,128)}, f32[32,16,128]{2,1,0:T(8,128)S(1)}, u32[]{:S(2)}) copy-start(f32[32,16,128]{2,1,0:T(8,128)S(1)} %copy.1632) | copy-start | bytes 786436
  104.7 20.8 %copy-start = (f32[14,16,16,128]{3,2,1,0:T(8,128)S(1)}, f32[14,16,16,128]{3,2,1,0:T(8,128)}, u32[]{:S(2)}) copy-start(f32[14,16,16,128]{3,2,1,0:T(8,128)} %constant_dynamic-update-slice_fusion.13) | copy-start | bytes 5505028
  138.7 18.9 %copy-start.1 = (f32[14,16,16,128]{3,2,1,0:T(8,128)S(1)}, f32[14,16,16,128]{3,2,1,0:T(8,128)}, u32[]{:S(2)}) copy-start(f32[14,16,16,128]{3,2,1,0:T(8,128)} %constant_dynamic-update-slice_fusion.69) | copy-start | bytes 5505028
  (161 other events, 198.9 us)
where the time goes:
time: 223 us; the launch traced here: 219 us
  other arithmetic  63.6 us (29%)
  blocking collectives  63.3 us (28%)
  local copies, waits for them, and re-layouts  57.4 us (26%)
  starting transfers between devices  18.6 us (8%)
  waiting for transfers between devices  10 us (4%)
  between operations  6 us (3%)
    all_gather x2, blocking collectives, coupled(): gathered = lax.all_gather(boundary[None], 'xs', axis=0, tiled=True)  39.2 us
    unnamed x80, other arithmetic  26.3 us
    unnamed x406, local copies, waits for them, and re-layouts  21.7 us
    all_to_all x1, blocking collectives, to_lines(): return lax.all_to_all(values, 'pl', split_axis=1, concat_axis=2, tiled=True)  12.3 us
    all_to_all x1, blocking collectives, to_planes(): return lax.all_to_all(values, 'pl', split_axis=2, concat_axis=1, tiled=True)  11.8 us
    add x2, other arithmetic, matrix_vector(): matrix[2] * vector[0] + matrix[3] * vector[1]  10.1 us
    slice x42, local copies, waits for them, and re-layouts, halves(): return (paired[..., 0], paired[..., 1])  9.86 us
    all_to_all x1, starting transfers between devices, shards(): lax.all_to_all(northward_rate, 'pl', split_axis=1, concat_axis=2, tiled=T...  7.38 us
  transfers between devices with their start and end apart: 3, of which 2 were waited for; matrix products, arithmetic and copies ran while one was open for 11% of the time, Pallas kernels for 0%

commit v1 on v0

--- a/solution.py
+++ b/solution.py
@@ -2,6 +2,13 @@
 import jax.numpy as jnp
 from jax import lax
 from jax.sharding import PartitionSpec as P
+
+
+def exchange_blocks(x, mesh_axis, split, join):
+    devices = lax.axis_size(mesh_axis)
+    pieces = jnp.stack(jnp.split(x, devices, axis=split), axis=0)
+    pieces = lax.all_to_all(pieces, mesh_axis, split_axis=0, concat_axis=0)
+    return jnp.concatenate(pieces, axis=join)
 
 
 def cyclic(sub_band, centre, super_band, values):
@@ -83,7 +90,7 @@
 
 
 def to_lines(values):
-    return lax.all_to_all(values, "pl", split_axis=1, concat_axis=2, tiled=True)
+    return exchange_blocks(values, "pl", 1, 2)
 
 
 def to_planes(values):

time: 223 us -> 232 us (1.040)
  local copies, waits for them, and re-layouts: 57.4 us -> 66 us
    unnamed x406 -> x428, local copies, waits for them, and re-layouts: 21.7 us -> 30.4 us
where the time goes in v1:
time: 232 us; the launch traced here: 228 us
  local copies, waits for them, and re-layouts  66 us (28%)
  other arithmetic  63.7 us (27%)
  blocking collectives  63.3 us (27%)
  starting transfers between devices  18.6 us (8%)
  waiting for transfers between devices  10.2 us (4%)
  between operations  6.2 us (3%)
    all_gather x2, blocking collectives, coupled(): gathered = lax.all_gather(boundary[None], 'xs', axis=0, tiled=True)  39.2 us
    unnamed x428, local copies, waits for them, and re-layouts  30.4 us
    unnamed x80, other arithmetic  26.3 us
    all_to_all x1, blocking collectives, exchange_blocks(): pieces = lax.all_to_all(pieces, mesh_axis, split_axis=0, concat_axis=0)  12.3 us
    all_to_all x1, blocking collectives, to_planes(): return lax.all_to_all(values, 'pl', split_axis=2, concat_axis=1, tiled=True)  11.8 us
    add x2, other arithmetic, matrix_vector(): matrix[2] * vector[0] + matrix[3] * vector[1]  10.1 us
    slice x42, local copies, waits for them, and re-layouts, halves(): return (paired[..., 0], paired[..., 1])  9.9 us
    all_to_all x1, starting transfers between devices, shards(): lax.all_to_all(northward_rate, 'pl', split_axis=1, concat_axis=2, tiled=T...  7.38 us
  transfers between devices with their start and end apart: 3, of which 2 were waited for; matrix products, arithmetic and copies ran while one was open for 11% of the time, Pallas kernels for 0%

profile of v1, /device:TPU:32, one launch (start us, length us, event | category | flops | bytes accessed | tf_op | source)
XLA Modules:
  0.0 228.0 jit_solution(1565510878924117892)
XLA Ops:
  13.0 7.0 %all-to-all-start = ((f32[16,32,1,128]{3,1,2,0:T(8,128)}), f32[16,32,1,128]{3,1,2,0:T(8,128)S(1)}, u32[]{:S(2)}, u32[]{:S(2)}) async-start(f32[16,32,1,128]{3,1,2,0:T(8,128)} %constant_dynamic-update-slice_fusion), calls=%async_computation | async-start | bytes 524288 | tf_op jit(solution)/shard_map/all_to_all | solution.py:10
  37.1 7.4 %all-to-all-start.1 = ((f32[32,16,128]{2,0,1:T(8,128)}), f32[32,16,128]{2,0,1:T(8,128)S(1)}, u32[]{:S(2)}, u32[]{:S(2)}) async-start(f32[32,16,128]{2,0,1:T(8,128)} %copy.1638), calls=%async_computation.1 | async-start | bytes 524288 | tf_op jit(solution)/shard_map/all_to_all | solution.py:264
  44.9 1.6 fusion.580
  47.3 5.9 %all-to-all-done.1 = f32[32,16,128]{2,0,1:T(8,128)S(1)} async-done(((f32[32,16,128]{2,0,1:T(8,128)}), f32[32,16,128]{2,0,1:T(8,128)S(1)}, u32[]{:S(2)}, u32[]{:S(2)}) %all-to-all-start.1) | async-done | bytes 262176 | tf_op jit(solution)/shard_map/all_to_all | solution.py:264
  53.6 1.6 fusion.579
  56.7 2.6 %copy_select_fusion = (f32[32,1,1024,2]{0,2,3,1:T(8,128)S(1)}, f32[32,1,1024,2]{0,2,3,1:T(8,128)S(1)}) fusion(f32[32,1,1024,2]{0,3,2,1:T(2,128)} %bitcast.4822, pred[1024,2]{0,1:T(4,128)(4,1)S(1)} %get-tuple-element.518, pred[1024,2]{0,1:T(4,128)(4,1)S(1)} %get-tuple-element.519), kind=kLoop, calls=%fused_computation.210 | loop fusion | flops 131072 | bytes 790528 | tf_op jit(solution)/shard_map/jit(_where)/select_n | solution.py:88
  71.3 1.9 copy.1716
  73.7 11.6 %reduce = f32[2048,32]{1,0:T(8,128)} reduce(f32[2048,1,32]{2,1,0:T(1,128)} %bitcast.4826, f32[]{:T(128)} %broadcast.2033), dimensions={1}, to_apply=%bitcast.4160.reduce_sub_computation | reduce | bytes 524292
  85.3 2.4 %reshape.3590 = f32[16,1,4096]{2,1,0:T(1,128)} reshape(f32[2048,32]{1,0:T(8,128)} %reduce) | data formatting | bytes 524288
  87.7 4.2 %all-to-all-start.2 = ((f32[16,1,4096]{2,1,0:T(1,128)}), f32[16,1,4096]{2,1,0:T(1,128)}, u32[]{:S(2)}, u32[]{:S(2)}) async-start(f32[16,1,4096]{2,1,0:T(1,128)} %reshape.3590), calls=%async_computation.2 | async-start | bytes 524288 | tf_op jit(solution)/shard_map/all_to_all | solution.py:97
  94.6 1.7 bitcast_divide_fusion.61
  96.3 4.3 %all-to-all-done.2 = f32[16,1,4096]{2,1,0:T(1,128)} async-done(((f32[16,1,4096]{2,1,0:T(1,128)}), f32[16,1,4096]{2,1,0:T(1,128)}, u32[]{:S(2)}, u32[]{:S(2)}) %all-to-all-start.2) | async-done | bytes 262176 | tf_op jit(solution)/shard_map/all_to_all | solution.py:97
  100.6 2.9 %reduce.1 = f32[16,4096]{1,0:T(8,128)} reduce(f32[16,1,4096]{2,1,0:T(1,128)} %all-to-all-done.2, f32[]{:T(128)} %broadcast.2033), dimensions={1}, to_apply=%all_to_all.14.reduce_sub_computation | reduce | bytes 524292 | tf_op jit(solution)/shard_map/all_to_all | solution.py:97
  103.5 3.8 %reshape.3591 = f32[2048,1,32]{2,1,0:T(1,128)} reshape(f32[16,4096]{1,0:T(8,128)} %reduce.1) | data formatting | bytes 524288
  107.3 3.4 %copy.1718 = f32[32,1,2048]{2,1,0:T(1,128)} copy(f32[32,1,2048]{0,1,2:T(1,128)} %bitcast.4823) | data formatting | bytes 524288 | tf_op jit(solution)/shard_map/all_to_all | solution.py:97
  114.5 20.5 %all-gather = f32[96,16,128]{2,1,0:T(8,128)S(1)} all-gather(f32[6,16,128]{2,1,0:T(8,128)S(1)} %constant_dynamic-update-slice_fusion.16), channel_id=2, replica_groups=mesh['pl'=16,'xs'=16] {'xs'}, dimensions={0}, use_global_device_ids=true | all-gather | bytes 835584 | tf_op jit(solution)/shard_map/all_gather | solution.py:222
  140.4 5.1 %fusion.406 = (f32[16,16,128]{2,1,0:T(8,128)S(1)}, f32[16,16,128]{2,1,0:T(8,128)S(1)}, f32[16,16,128]{2,1,0:T(8,128)S(1)}, f32[16,16,128]{2,1,0:T(8,128)S(1)}, f...) fusion(f32[16,16,128]{2,1,0:T(8,128)S(1)} %get-tuple-element.322, ...), kind=kLoop, calls=%fused_computation.1307 | loop fusion | flops 23101440 | bytes 16613376 | tf_op jit(solution)/shard_map/add | solution.py:122
  147.5 18.6 %all-gather.1 = f32[96,16,128]{2,1,0:T(8,128)S(1)} all-gather(f32[6,16,128]{2,1,0:T(8,128)S(1)} %constant_dynamic-update-slice_fusion.74), channel_id=3, replica_groups=mesh['pl'=16,'xs'=16] {'xs'}, dimensions={0}, use_global_device_ids=true | all-gather | bytes 835584 | tf_op jit(solution)/shard_map/all_gather | solution.py:222
  171.6 5.0 %fusion.403 = (f32[16,16,128]{2,1,0:T(8,128)S(1)}, f32[16,16,128]{2,1,0:T(8,128)S(1)}, f32[16,16,128]{2,1,0:T(8,128)S(1)}, f32[16,16,128]{2,1,0:T(8,128)S(1)}, f...) fusion(f32[16,16,128]{2,1,0:T(8,128)S(1)} %get-tuple-element.316, ...), kind=kLoop, calls=%fused_computation.1215 | loop fusion | flops 23101440 | bytes 16613376 | tf_op jit(solution)/shard_map/add | solution.py:122
  177.2 12.3 %all_to_all.40 = f32[16,32,1,128]{3,1,2,0:T(8,128)S(1)} all-to-all(f32[16,32,1,128]{3,1,2,0:T(8,128)S(1)} %constant_dynamic-update-slice_fusion.132), channel_id=1, replica_groups=mesh['pl'=16,'xs'=16] {'pl'}, dimensions={0} | all-to-all | bytes 524288 | tf_op jit(solution)/shard_map/all_to_all | solution.py:10
  190.8 2.6 %fusion.578 = (f32[32,1,1024,1]{0,3,2,1:T(1,128)S(1)}, f32[32,1,1024,1]{0,3,2,1:T(1,128)S(1)}) fusion(f32[32,1,1024,2]{0,3,2,1:T(2,128)} %bitcast.4827), kind=kLoop, calls=%fused_computation.1811 | loop fusion | bytes 524288 | tf_op jit(solution)/shard_map/slice | solution.py:50
  199.7 9.3 %reduce.2 = f32[2048,32]{1,0:T(8,128)S(1)} reduce(f32[2048,1,32]{2,1,0:T(1,128)S(1)} %bitcast.4828, f32[]{:T(128)} %broadcast.2033), dimensions={1}, to_apply=%bitcast.4162.reduce_sub_computation | reduce | bytes 524292
  209.5 11.8 %all_to_all.41 = f32[16,1,4096]{2,1,0:T(1,128)S(1)} all-to-all(f32[16,1,4096]{2,1,0:T(1,128)S(1)} %reshape.3592), channel_id=1, replica_groups=mesh['pl'=16,'xs'=16] {'pl'}, dimensions={0} | all-to-all | bytes 524288 | tf_op jit(solution)/shard_map/all_to_all | solution.py:97
  222.5 1.8 reshape.3593
  (918 shorter events, 72.4 us)
Async XLA Ops:
  3.0 17.1 %copy-start.109 = (f32[32,16,128]{2,1,0:T(8,128)S(1)}, f32[32,16,128]{2,1,0:T(8,128)}, u32[]{:S(2)}) copy-start(f32[32,16,128]{2,1,0:T(8,128)} %param.6) | copy-start | bytes 786436
  13.0 24.2 %all-to-all-start = ((f32[16,32,1,128]{3,1,2,0:T(8,128)}), f32[16,32,1,128]{3,1,2,0:T(8,128)S(1)}, u32[]{:S(2)}, u32[]{:S(2)}) async-start(f32[16,32,1,128]{3,1,2,0:T(8,128)} %constant_dynamic-update-slice_fusion), calls=%async_computation | async-start | bytes 524288 | tf_op jit(solution)/shard_map/all_to_all | solution.py:10
  22.9 12.8 %copy-start.108 = (f32[32,16,128]{2,1,0:T(8,128)S(1)}, f32[32,16,128]{2,1,0:T(8,128)}, u32[]{:S(2)}) copy-start(f32[32,16,128]{2,1,0:T(8,128)} %param.7) | copy-start | bytes 786436
  37.1 16.1 %all-to-all-start.1 = ((f32[32,16,128]{2,0,1:T(8,128)}), f32[32,16,128]{2,0,1:T(8,128)S(1)}, u32[]{:S(2)}, u32[]{:S(2)}) async-start(f32[32,16,128]{2,0,1:T(8,128)} %copy.1638), calls=%async_computation.1 | async-start | bytes 524288 | tf_op jit(solution)/shard_map/all_to_all | solution.py:264
  62.3 8.1 %copy-start.2 = (f32[32,1,512,1]{0,3,2,1:T(1,128)}, f32[32,1,512,1]{0,3,2,1:T(1,128)S(1)}, u32[]{:S(2)}) copy-start(f32[32,1,512,1]{0,3,2,1:T(1,128)S(1)} %get-tuple-element.347) | copy-start | bytes 196612
  62.8 7.6 %copy-start.4 = (f32[32,1,512,1]{0,3,2,1:T(1,128)}, f32[32,1,512,1]{0,3,2,1:T(1,128)S(1)}, u32[]{:S(2)}) copy-start(f32[32,1,512,1]{0,3,2,1:T(1,128)S(1)} %get-tuple-element.343) | copy-start | bytes 196612
  64.1 5.9 %copy-start.16 = (f32[32,1,256,1]{0,3,2,1:T(1,128)}, f32[32,1,256,1]{0,3,2,1:T(1,128)S(1)}, u32[]{:S(2)}) copy-start(f32[32,1,256,1]{0,3,2,1:T(1,128)S(1)} %get-tuple-element.388) | copy-start | bytes 98308
  64.4 5.7 %copy-start.18 = (f32[32,1,256,1]{0,3,2,1:T(1,128)}, f32[32,1,256,1]{0,3,2,1:T(1,128)S(1)}, u32[]{:S(2)}) copy-start(f32[32,1,256,1]{0,3,2,1:T(1,128)S(1)} %get-tuple-element.384) | copy-start | bytes 98308
  64.8 5.0 %copy-start.14 = (f32[32,1,128,1]{0,3,2,1:T(1,128)}, f32[32,1,128,1]{0,3,2,1:T(1,128)S(1)}, u32[]{:S(2)}) copy-start(f32[32,1,128,1]{0,3,2,1:T(1,128)S(1)} %get-tuple-element.415) | copy-start | bytes 49156
  65.2 4.6 %copy-start.37 = (f32[32,1,128,1]{0,3,2,1:T(1,128)}, f32[32,1,128,1]{0,3,2,1:T(1,128)S(1)}, u32[]{:S(2)}) copy-start(f32[32,1,128,1]{0,3,2,1:T(1,128)S(1)} %get-tuple-element.416) | copy-start | bytes 49156
  65.3 4.5 %copy-start.39 = (f32[32,1,128,1]{0,3,2,1:T(1,128)}, f32[32,1,128,1]{0,3,2,1:T(1,128)S(1)}, u32[]{:S(2)}) copy-start(f32[32,1,128,1]{0,3,2,1:T(1,128)S(1)} %get-tuple-element.412) | copy-start | bytes 49156
  65.6 4.0 %copy-start.31 = (f32[32,1,64,1]{0,3,2,1:T(1,128)}, f32[32,1,64,1]{0,3,2,1:T(1,128)S(1)}, u32[]{:S(2)}) copy-start(f32[32,1,64,1]{0,3,2,1:T(1,128)S(1)} %get-tuple-element.433) | copy-start | bytes 24580
  66.1 3.6 %copy-start.63 = (f32[32,1,64,1]{0,3,2,1:T(1,128)}, f32[32,1,64,1]{0,3,2,1:T(1,128)S(1)}, u32[]{:S(2)}) copy-start(f32[32,1,64,1]{0,3,2,1:T(1,128)S(1)} %get-tuple-element.434) | copy-start | bytes 24580
  66.1 3.6 %copy-start.67 = (f32[32,1,64,1]{0,3,2,1:T(1,128)}, f32[32,1,64,1]{0,3,2,1:T(1,128)S(1)}, u32[]{:S(2)}) copy-start(f32[32,1,64,1]{0,3,2,1:T(1,128)S(1)} %get-tuple-element.435) | copy-start | bytes 24580
  66.2 3.7 %copy-start.65 = (f32[32,1,64,1]{0,3,2,1:T(1,128)}, f32[32,1,64,1]{0,3,2,1:T(1,128)S(1)}, u32[]{:S(2)}) copy-start(f32[32,1,64,1]{0,3,2,1:T(1,128)S(1)} %get-tuple-element.430) | copy-start | bytes 24580
  66.2 3.7 %copy-start.96 = (f32[32,1,64]{0,2,1:T(8,128)}, f32[32,1,64]{0,2,1:T(8,128)S(1)}, u32[]{:S(2)}) copy-start(f32[32,1,64]{0,2,1:T(8,128)S(1)} %get-tuple-element.236) | copy-start | bytes 24580
  66.4 3.1 %copy-start.80 = (f32[32,1,32,1]{0,3,2,1:T(1,128)}, f32[32,1,32,1]{0,3,2,1:T(1,128)S(1)}, u32[]{:S(2)}) copy-start(f32[32,1,32,1]{0,3,2,1:T(1,128)S(1)} %get-tuple-element.449) | copy-start | bytes 12292
  66.4 3.2 %copy-start.84 = (f32[32,1,32,1]{0,3,2,1:T(1,128)}, f32[32,1,32,1]{0,3,2,1:T(1,128)S(1)}, u32[]{:S(2)}) copy-start(f32[32,1,32,1]{0,3,2,1:T(1,128)S(1)} %get-tuple-element.450) | copy-start | bytes 12292
  66.5 3.0 %copy-start.82 = (f32[32,1,32,1]{0,3,2,1:T(1,128)}, f32[32,1,32,1]{0,3,2,1:T(1,128)S(1)}, u32[]{:S(2)}) copy-start(f32[32,1,32,1]{0,3,2,1:T(1,128)S(1)} %get-tuple-element.445) | copy-start | bytes 12292
  73.7 18.9 %copy-start.56 = (f32[16,1,1,16,128]{4,1,0,3,2:T(1,128)S(1)}, f32[16,1,1,16,128]{4,1,0,3,2:T(1,128)}, u32[]{:S(2)}) copy-start(f32[16,1,1,16,128]{4,1,0,3,2:T(1,128)} %copy-done.55) | copy-start | bytes 393220
  73.7 19.6 %copy-start.60 = (f32[32,16,128]{2,0,1:T(8,128)S(1)}, f32[32,16,128]{2,0,1:T(8,128)}, u32[]{:S(2)}) copy-start(f32[32,16,128]{2,0,1:T(8,128)} %get-tuple-element.380) | copy-start | bytes 786436
  87.7 12.9 %all-to-all-start.2 = ((f32[16,1,4096]{2,1,0:T(1,128)}), f32[16,1,4096]{2,1,0:T(1,128)}, u32[]{:S(2)}, u32[]{:S(2)}) async-start(f32[16,1,4096]{2,1,0:T(1,128)} %reshape.3590), calls=%async_computation.2 | async-start | bytes 524288 | tf_op jit(solution)/shard_map/all_to_all | solution.py:97
  114.3 20.8 %copy-start = (f32[14,16,16,128]{3,2,1,0:T(8,128)S(1)}, f32[14,16,16,128]{3,2,1,0:T(8,128)}, u32[]{:S(2)}) copy-start(f32[14,16,16,128]{3,2,1,0:T(8,128)} %constant_dynamic-update-slice_fusion.31) | copy-start | bytes 5505028
  147.4 18.9 %copy-start.1 = (f32[14,16,16,128]{3,2,1,0:T(8,128)S(1)}, f32[14,16,16,128]{3,2,1,0:T(8,128)}, u32[]{:S(2)}) copy-start(f32[14,16,16,128]{3,2,1,0:T(8,128)} %constant_dynamic-update-slice_fusion.89) | copy-start | bytes 5505028
  (157 other events, 196.2 us)
